TPU v7x, 32 devices: a whole 2x2x4 slice. The times are simulated.
32 devices in a mesh: fsdp: 8 (over z, x), seq: 4 (over y, core).
Axes of the slice: x: 2, y: 2, z: 4, core: 2. Of those that a mesh axis runs over, the one named last changes fastest.
Arguments:
- residual: bfloat16 [24, 1024, 767], P('fsdp', 'seq'), may hold values from -6 to 6
- out_grad: bfloat16 [24, 1024, 767], P('fsdp', 'seq'), may hold values from -6 to 6
- doc_lengths: int32 [24, 8], P('fsdp'), may hold values from 1 to 512, 1024 in all within a row
- gain_one: float32 [768], replicated, may hold values from 0.5 to 1.5
- qkv_weight: float32 [768, 2304], P('fsdp'), may hold values from -0.21875 to 0.21875
- qv_bias: float32 [12, 128], replicated, may hold values from -3 to 3
- out_weight: float32 [768, 767], P('fsdp'), may hold values from -0.875 to 0.875
- out_bias: float32 [767], replicated, may hold values from -3 to 3
- gain_two: float32 [768], replicated, may hold values from 0.5 to 1.5
- fc_weight: float32 [768, 3072], P('fsdp'), may hold values from -0.21875 to 0.21875
- fc_bias: float32 [3072], replicated, may hold values from -3 to 3
- proj_weight: float32 [3072, 767], P('fsdp'), may hold values from -0.15625 to 0.15625
- proj_bias: float32 [767], replicated, may hold values from -3 to 3
Outputs:
- output: bfloat16 [24, 1024, 767], P('fsdp', 'seq')
- input_grad: float32 [24, 1024, 767], P('fsdp', 'seq')
- gain_one_grad: float32 [768], replicated
- qkv_weight_grad: float32 [768, 2304], P('fsdp')
- qv_bias_grad: float32 [12, 128], replicated
- out_weight_grad: float32 [768, 767], P('fsdp')
- out_bias_grad: float32 [767], replicated
- gain_two_grad: float32 [768], replicated
- fc_weight_grad: float32 [768, 3072], P('fsdp')
- fc_bias_grad: float32 [3072], replicated
- proj_weight_grad: float32 [3072, 767], P('fsdp')
- proj_bias_grad: float32 [767], replicated
Inputs may be any that keep to these rules, and one draw needn't show every extreme that they name: `doc_lengths`: each sequence's 8 document lengths sum to 1024; the longest is exactly 512 tokens.
All inputs are finite; a program needn't handle non-finite values.
Results may differ from a plain program's by a relative error of at most 0.014.
Values may be sent and summed in bfloat16 or wider, within the bound.
No kernel may reach another device: no remote copies, remote signals or barrier semaphores. Data moves between devices by JAX's collectives and lax.ppermute only.
A program may use at most 320 MiB of HBM per device.

v0:
```python
import functools
import jax
import jax.numpy as jnp
from jax import lax
from jax.sharding import PartitionSpec as P

EPS = 1e-06


def centred_norm(residual, gain):
    row_total = jnp.sum(residual, axis=-1, keepdims=True)
    full_row = jnp.concatenate([residual, -row_total], axis=-1)
    inv_rms = lax.rsqrt(jnp.mean(full_row * full_row, axis=-1, keepdims=True) + EPS)
    return full_row * inv_rms * gain


def document_index(lengths, length):
    starts = jnp.cumsum(lengths, axis=1) - lengths
    position = jnp.arange(length, dtype=jnp.int32)
    inside = (position[None, :, None] >= starts[:, None, :]).astype(jnp.int32)
    return jnp.sum(inside, axis=2) - 1


def masked_scores(queries, key_rows, doc_ids, first_row, row_count, factor):
    scores = factor * jnp.einsum(
        "bqhe,bkhe->bhqk", queries, key_rows, preferred_element_type=jnp.float32
    )
    length = key_rows.shape[1]
    row_pos = first_row + jnp.arange(row_count, dtype=jnp.int32)
    col_pos = jnp.arange(length, dtype=jnp.int32)
    row_ids = doc_ids[:, first_row : first_row + row_count]
    allowed = (row_ids[:, :, None] == doc_ids[:, None, :]) & (
        col_pos[None, None, :] <= row_pos[None, :, None]
    )
    return jnp.where(allowed[:, None], scores, -1e30)


def local(
    residual,
    out_grad,
    doc_lengths,
    gain_one,
    qkv_weight,
    qv_bias,
    out_weight,
    out_bias,
    gain_two,
    fc_weight,
    fc_bias,
    proj_weight,
    proj_bias,
):
    ranks = lax.axis_size("seq")
    seq_count, local_len, narrow = residual.shape
    width = narrow + 1
    full_len = local_len * ranks
    heads_all = qv_bias.shape[0]
    head_dim = qv_bias.shape[1] // 2
    my_heads = heads_all // ranks
    token_count = seq_count * local_len
    factor = head_dim ** (-0.5)
    block_rows = min(512, full_len)
    qkv_matrix, out_matrix, fc_matrix, proj_matrix = (
        lax.all_gather(qkv_weight.astype(jnp.bfloat16), "fsdp", axis=0, tiled=True),
        lax.all_gather(out_weight.astype(jnp.bfloat16), "fsdp", axis=0, tiled=True),
        lax.all_gather(fc_weight.astype(jnp.bfloat16), "fsdp", axis=0, tiled=True),
        lax.all_gather(proj_weight.astype(jnp.bfloat16), "fsdp", axis=0, tiled=True),
    )
    resid_flat = residual.astype(jnp.float32).reshape(token_count, narrow)
    normed_one = centred_norm(resid_flat, gain_one).astype(jnp.bfloat16)
    zero_part = jnp.zeros((heads_all, head_dim), jnp.float32)
    bias_full = jnp.stack(
        [qv_bias[:, :head_dim], zero_part, qv_bias[:, head_dim:]], axis=1
    ).reshape(3 * width)
    packed = (
        jnp.dot(normed_one, qkv_matrix, preferred_element_type=jnp.float32) + bias_full
    ).astype(jnp.bfloat16)
    packed = packed.reshape(seq_count, local_len, ranks, my_heads * 3 * head_dim)
    by_heads = lax.all_to_all(packed, "seq", split_axis=2, concat_axis=1, tiled=True)
    by_heads = by_heads.reshape(seq_count, full_len, my_heads, 3, head_dim)
    queries = by_heads[:, :, :, 0]
    key_rows = by_heads[:, :, :, 1]
    value_rows = by_heads[:, :, :, 2]
    doc_ids = document_index(doc_lengths, full_len)
    outputs_list = []
    lse_list = []
    for first_row in range(0, full_len, block_rows):
        scores = masked_scores(
            queries[:, first_row : first_row + block_rows],
            key_rows,
            doc_ids,
            first_row,
            block_rows,
            factor,
        )
        row_max = jnp.max(scores, axis=-1, keepdims=True)
        exp_scores = jnp.exp(scores - row_max)
        row_total = jnp.sum(exp_scores, axis=-1, keepdims=True)
        prob_low = (exp_scores / row_total).astype(jnp.bfloat16)
        lse_list.append(row_max + jnp.log(row_total))
        outputs_list.append(
            jnp.einsum("bhqk,bkhe->bqhe", prob_low, value_rows, preferred_element_type=jnp.float32)
        )
    attended = jnp.concatenate(outputs_list, axis=1).astype(jnp.bfloat16)
    attended = attended.reshape(seq_count, full_len, my_heads * head_dim)
    by_tokens = lax.all_to_all(attended, "seq", split_axis=1, concat_axis=2, tiled=True)
    attn_flat = by_tokens.reshape(token_count, width)
    middle = (
        resid_flat + jnp.dot(attn_flat, out_matrix, preferred_element_type=jnp.float32) + out_bias
    )
    normed_two = centred_norm(middle, gain_two).astype(jnp.bfloat16)
    pre_act = jnp.dot(normed_two, fc_matrix, preferred_element_type=jnp.float32) + fc_bias
    hidden = jax.nn.gelu(pre_act, approximate=True).astype(jnp.bfloat16)
    output = middle + jnp.dot(hidden, proj_matrix, preferred_element_type=jnp.float32) + proj_bias
    output = output.astype(jnp.bfloat16).reshape(seq_count, local_len, narrow)
    qkv_matrix, out_matrix, fc_matrix, proj_matrix = (
        lax.all_gather(qkv_weight.astype(jnp.bfloat16), "fsdp", axis=0, tiled=True),
        lax.all_gather(out_weight.astype(jnp.bfloat16), "fsdp", axis=0, tiled=True),
        lax.all_gather(fc_weight.astype(jnp.bfloat16), "fsdp", axis=0, tiled=True),
        lax.all_gather(proj_weight.astype(jnp.bfloat16), "fsdp", axis=0, tiled=True),
    )
    grad_low = out_grad.reshape(token_count, narrow)
    grad_flat = grad_low.astype(jnp.float32)
    proj_grad = jnp.einsum("tf,tc->fc", hidden, grad_low, preferred_element_type=jnp.float32)
    proj_bias_grad = jnp.sum(grad_flat, axis=0)
    d_hidden = jnp.einsum("tc,fc->tf", grad_low, proj_matrix, preferred_element_type=jnp.float32)
    gelu_value, gelu_back = jax.vjp(functools.partial(jax.nn.gelu, approximate=True), pre_act)
    d_pre = gelu_back(d_hidden)[0].astype(jnp.bfloat16)
    fc_grad = jnp.einsum("td,tf->df", normed_two, d_pre, preferred_element_type=jnp.float32)
    fc_bias_grad = jnp.sum(d_pre.astype(jnp.float32), axis=0)
    d_norm_two = jnp.einsum("tf,df->td", d_pre, fc_matrix, preferred_element_type=jnp.float32)
    second_value, second_back = jax.vjp(centred_norm, middle, gain_two)
    d_mid_part, gain_two_grad = second_back(d_norm_two)
    d_middle = grad_flat + d_mid_part
    d_branch = d_middle.astype(jnp.bfloat16)
    out_weight_part = jnp.einsum(
        "td,tc->dc", attn_flat, d_branch, preferred_element_type=jnp.float32
    )
    out_bias_grad = jnp.sum(d_branch.astype(jnp.float32), axis=0)
    d_attn = jnp.einsum(
        "tc,dc->td", d_branch, out_matrix, preferred_element_type=jnp.float32
    ).astype(jnp.bfloat16)
    d_attn = d_attn.reshape(seq_count, local_len, ranks, my_heads * head_dim)
    d_heads = lax.all_to_all(d_attn, "seq", split_axis=2, concat_axis=1, tiled=True)
    d_heads = d_heads.reshape(seq_count, full_len, my_heads, head_dim)
    key_grad = jnp.zeros((seq_count, full_len, my_heads, head_dim), jnp.float32)
    value_grad = jnp.zeros((seq_count, full_len, my_heads, head_dim), jnp.float32)
    query_parts = []
    for block_index, first_row in enumerate(range(0, full_len, block_rows)):
        query_block = queries[:, first_row : first_row + block_rows]
        grad_block = d_heads[:, first_row : first_row + block_rows]
        scores = masked_scores(query_block, key_rows, doc_ids, first_row, block_rows, factor)
        prob_full = jnp.exp(scores - lse_list[block_index])
        prob_low = prob_full.astype(jnp.bfloat16)
        d_probs = jnp.einsum(
            "bqhe,bkhe->bhqk", grad_block, value_rows, preferred_element_type=jnp.float32
        )
        row_delta = jnp.sum(prob_full * d_probs, axis=-1, keepdims=True)
        d_scores = (prob_full * (d_probs - row_delta)).astype(jnp.bfloat16)
        query_parts.append(
            factor
            * jnp.einsum("bhqk,bkhe->bqhe", d_scores, key_rows, preferred_element_type=jnp.float32)
        )
        key_grad = key_grad + factor * jnp.einsum(
            "bhqk,bqhe->bkhe", d_scores, query_block, preferred_element_type=jnp.float32
        )
        value_grad = value_grad + jnp.einsum(
            "bhqk,bqhe->bkhe", prob_low, grad_block, preferred_element_type=jnp.float32
        )
    query_grad = jnp.concatenate(query_parts, axis=1)
    d_packed = jnp.stack([query_grad, key_grad, value_grad], axis=3).astype(jnp.bfloat16)
    d_packed = d_packed.reshape(seq_count, full_len, my_heads * 3 * head_dim)
    d_tokens = lax.all_to_all(d_packed, "seq", split_axis=1, concat_axis=2, tiled=True)
    d_tokens = d_tokens.reshape(token_count, 3 * width)
    qkv_grad = jnp.einsum("td,tc->dc", normed_one, d_tokens, preferred_element_type=jnp.float32)
    column_sums = jnp.sum(d_tokens.astype(jnp.float32), axis=0).reshape(heads_all, 3, head_dim)
    qv_bias_grad = jnp.concatenate([column_sums[:, 0], column_sums[:, 2]], axis=1)
    d_norm_one = jnp.einsum("tc,dc->td", d_tokens, qkv_matrix, preferred_element_type=jnp.float32)
    first_value, first_back = jax.vjp(centred_norm, resid_flat, gain_one)
    d_resid_part, gain_one_grad = first_back(d_norm_one)
    input_grad = (d_middle + d_resid_part).reshape(seq_count, local_len, narrow)
    qkv_share, out_share, fc_share, proj_share = (
        lax.psum_scatter(qkv_grad, "fsdp", scatter_dimension=0, tiled=True),
        lax.psum_scatter(out_weight_part, "fsdp", scatter_dimension=0, tiled=True),
        lax.psum_scatter(fc_grad, "fsdp", scatter_dimension=0, tiled=True),
        lax.psum_scatter(proj_grad, "fsdp", scatter_dimension=0, tiled=True),
    )
    qkv_share, out_share, fc_share, proj_share = (
        lax.psum(qkv_share.astype(jnp.bfloat16), "seq").astype(jnp.float32),
        lax.psum(out_share.astype(jnp.bfloat16), "seq").astype(jnp.float32),
        lax.psum(fc_share.astype(jnp.bfloat16), "seq").astype(jnp.float32),
        lax.psum(proj_share.astype(jnp.bfloat16), "seq").astype(jnp.float32),
    )
    vector_sums = lax.psum(
        (gain_one_grad, qv_bias_grad, out_bias_grad, gain_two_grad, fc_bias_grad, proj_bias_grad),
        ("fsdp", "seq"),
    )
    return (
        output,
        input_grad,
        vector_sums[0],
        qkv_share,
        vector_sums[1],
        out_share,
        vector_sums[2],
        vector_sums[3],
        fc_share,
        vector_sums[4],
        proj_share,
        vector_sums[5],
    )


def solution(mesh):
    return jax.shard_map(
        local,
        mesh=mesh,
        in_specs=(
            P("fsdp", "seq", None),
            P("fsdp", "seq", None),
            P("fsdp", None),
            P(),
            P("fsdp", None),
            P(),
            P("fsdp", None),
            P(),
            P(),
            P("fsdp", None),
            P(),
            P("fsdp", None),
            P(),
        ),
        out_specs=(
            P("fsdp", "seq", None),
            P("fsdp", "seq", None),
            P(),
            P("fsdp", None),
            P(),
            P("fsdp", None),
            P(),
            P(),
            P("fsdp", None),
            P(),
            P("fsdp", None),
            P(),
        ),
        check_vma=False,
    )
```

profile of v0, /device:TPU:0, one launch (start us, length us, event | category | flops | bytes accessed | tf_op | source)
XLA Modules:
  0.0 1041.5 jit_solution(17890892516380688609)
XLA Ops:
  15.6 63.1 %all-gather.5.cloned.1.call-done = bf16[768,2304]{1,0:T(8,128)(2,1)} async-done(((bf16[96,2304]{1,0:T(8,128)(2,1)}), bf16[768,2304]{1,0:T(8,128)(2,1)}) %all-gather.5.cloned.1.call-update) | async-done | bytes 3538960 | tf_op jit(solution)/shard_map/all_gather | solution.py:64
  78.7 6.6 add_convert_fusion
  85.3 9.1 reshape.215
  94.4 7.9 copy.69
  102.3 3.8 all-to-all-start
  109.2 3.8 compare_and_fusion.1
  113.0 34.3 %all-to-all-done = bf16[3,256,4,576]{1,3,0,2:T(8,128)(2,1)S(1)} async-done(((bf16[3,256,4,576]{1,3,0,2:T(8,128)(2,1)}), bf16[3,256,4,576]{1,3,0,2:T(8,128)(2,1)S(1)}, u32[]{:S(2)}, u32[]{:S(2)}) %all-to-all-start) | async-done | bytes 3538976 | tf_op jit(solution)/shard_map/all_to_all | solution.py:79
  147.2 4.5 copy.70
  151.8 6.1 reshape.216
  159.8 9.2 fusion.57
  169.0 10.1 fusion.1
  179.0 9.0 fusion.28
  190.7 10.6 %fusion.58 = (f32[3,3,512]{2,1,0:T(4,128)}, f32[3,3,512,1024]{3,2,1,0:T(8,128)}) fusion(bf16[3,1024,3,3,64]{1,4,3,2,0:T(8,128)(2,1)S(1)} %reshape.216, bf16[3,1024,3,64]{1,3,2,0:T(8,128)(2,1)} %copy-done.13, pred[3,512,1024]{2,1,0:T(8,128)(4,1)} %get-tuple-element.34), kind=kOutput, calls=%fused_computation.122 | convolution fusion | flops 618130944 | bytes 22235136 | tf_op jit(solution)/shard_map/bqhe,bkhe->bhqk/dot_general | solution.py:25
  201.3 10.0 fusion
  211.3 9.0 fusion.29
  225.7 28.3 %all_to_all.60 = bf16[3,1024,192]{2,0,1:T(4,128)(2,1)S(1)} all-to-all(bf16[3,1024,192]{2,0,1:T(4,128)(2,1)S(1)} %pad_maximum_fusion.3), channel_id=1, replica_groups=mesh['fsdp'=8,'seq'=4] {'seq'}, dimensions={1} | all-to-all | bytes 2359296 | tf_op jit(solution)/shard_map/all_to_all | solution.py:106
  256.6 4.0 reshape.217
  265.6 10.9 %fusion.51 = f32[768,3072]{1,0:T(8,128)} fusion(bf16[768,3072]{1,0:T(8,128)(2,1)} %all-gather.9.cloned.1.call-done, f32[768]{0:T(1024)S(1)} %copy-done.25, f32[768]{0:T(1024)S(1)} %fusion.48, f32[768,1]{1,0:T(8,128)} %copy-done.11, f32[768,767]{1,0:T(8,128)} %copy-done.4), kind=kOutput, calls=%fused_computation.117 | convolution fusion | flops 3626237952 | bytes 16521216 | tf_op jit(solution)/shard_map/dot_general | solution.py:112
  276.5 5.5 all-gather.11.cloned.1.call-done
  282.0 13.7 %convert_reduce_fusion = (f32[3072]{0:T(1024)}, bf16[768,3072]{1,0:T(8,128)(2,1)S(1)}) fusion(f32[768,3072]{1,0:T(8,128)} %fusion.51, f32[3072]{0:T(1024)} %param.23, bf16[768,767]{1,0:T(8,128)(2,1)} %bitcast.116, bf16[3072,767]{1,0:T(8,128)(2,1)} %all-gather.11.cloned.1.call-done), kind=kOutput, calls=%fused_computation.27 | convolution fusion | flops 3673420800 | bytes 20070912 | tf_op jit(solution)/shard_map/tc,fc->tf/dot_general | solution.py:126
  295.7 4.8 multiply_reduce_fusion.2
  306.0 4.4 reshape.220
  310.4 3.5 copy.79
  314.0 4.3 all-to-all-start.2
  321.1 4.1 fusion.60
  325.3 8.9 all-to-all-done.2
  334.2 3.2 copy.80
  337.4 3.8 reshape.221
  341.2 8.6 fusion.11
  349.9 15.6 %multiply_reduce_fusion = (f32[3,3,512]{2,1,0:T(4,128)S(1)}, f32[3,3,512,1024]{3,2,1,0:T(8,128)}) fusion(f32[3,3,512,1024]{3,2,1,0:T(8,128)} %get-tuple-element.41, f32[3,3,512]{2,1,0:T(4,128)S(1)} %copy-done.21, bf16[3,1024,3,3,64]{1,4,3,2,0:T(8,128)(2,1)S(1)} %reshape.216, bf16[3,1024,3,64]{1,3,2,0:T(8,128)(2,1)S(1)} %copy-done.8), kind=kOutput, calls=%fused_computation.1 | convolution fusion | flops 618130944 | bytes 39561216 | tf_op jit(solution)/shard_map/bqhe,bkhe->bhqk/dot_general | solution.py:155
  365.5 15.5 %multiply_reduce_fusion.1 = (f32[3,3,512]{2,1,0:T(4,128)S(1)}, f32[3,3,512,1024]{3,2,1,0:T(8,128)}) fusion(f32[3,3,512,1024]{3,2,1,0:T(8,128)} %get-tuple-element.43, f32[3,3,512]{2,1,0:T(4,128)S(1)} %copy-done.22, bf16[3,1024,3,3,64]{1,4,3,2,0:T(8,128)(2,1)S(1)} %reshape.216, bf16[3,1024,3,64]{1,3,2,0:T(8,128)(2,1)S(1)} %copy-done.8), kind=kOutput, calls=%fused_computation.4 | convolution fusion | flops 618130944 | bytes 39561216 | tf_op jit(solution)/shard_map/bqhe,bkhe->bhqk/dot_general | solution.py:155
  381.0 13.1 %multiply_convert_fusion.1 = bf16[3,3,512,1024]{3,2,1,0:T(8,128)(2,1)S(1)} fusion(f32[3,3,512,1024]{3,2,1,0:T(8,128)} %get-tuple-element.48, f32[3,3,512,1024]{3,2,1,0:T(8,128)} %get-tuple-element.43, f32[3,3,512]{2,1,0:T(4,128)S(1)} %get-tuple-element.47, f32[3,3,512]{2,1,0:T(4,128)S(1)} %copy-done.22), kind=kLoop, calls=%fused_computation.3 | loop fusion | flops 18874368 | bytes 47222784 | tf_op jit(solution)/shard_map/convert_element_type | solution.py:159
  399.0 8.3 fusion.24
  407.2 13.1 %multiply_convert_fusion = bf16[3,3,512,1024]{3,2,1,0:T(8,128)(2,1)S(1)} fusion(f32[3,3,512,1024]{3,2,1,0:T(8,128)} %get-tuple-element.50, f32[3,3,512,1024]{3,2,1,0:T(8,128)} %get-tuple-element.41, f32[3,3,512]{2,1,0:T(4,128)S(1)} %get-tuple-element.49, f32[3,3,512]{2,1,0:T(4,128)S(1)} %copy-done.21), kind=kLoop, calls=%fused_computation | loop fusion | flops 18874368 | bytes 47222784 | tf_op jit(solution)/shard_map/convert_element_type | solution.py:159
  426.2 6.2 copy.82
  432.4 63.3 %all_to_all.61 = bf16[3,1024,576]{2,0,1:T(4,128)(2,1)S(1)} all-to-all(bf16[3,1024,576]{2,0,1:T(4,128)(2,1)} %copy.82), channel_id=1, replica_groups=mesh['fsdp'=8,'seq'=4] {'seq'}, dimensions={1} | all-to-all | bytes 7077888 | tf_op jit(solution)/shard_map/all_to_all | solution.py:173
  495.7 6.6 convert_reduce_fusion.1
  502.3 8.0 reshape.222
  510.3 7.6 fusion.49
  519.2 13.5 %fusion.52 = f32[3072,767]{1,0:T(8,128)} fusion(bf16[768,767]{1,0:T(8,128)(2,1)S(1)} %bitcast.117, f32[768,3072]{1,0:T(8,128)} %fusion.51, f32[3072]{0:T(1024)} %param.23), kind=kOutput, calls=%fused_computation.118 | convolution fusion | flops 3642753024 | bytes 20052480 | tf_op jit(solution)/shard_map/tf,tc->fc/dot_general | solution.py:124
  532.8 10.8 %fusion.50 = f32[768,3072]{1,0:T(8,128)} fusion(bf16[768,3072]{1,0:T(8,128)(2,1)} %copy-done.15, f32[768]{0:T(1024)S(1)} %copy-done.25, f32[768]{0:T(1024)S(1)} %fusion.48, f32[768,1]{1,0:T(8,128)} %copy-done.11, f32[768,767]{1,0:T(8,128)} %copy-done.4), kind=kOutput, calls=%fused_computation.116 | convolution fusion | flops 3626237952 | bytes 16521216 | tf_op jit(solution)/shard_map/td,tf->df/dot_general | solution.py:129
  544.8 12.8 %add_convert_fusion.2 = bf16[768,767]{1,0:T(8,128)(2,1)} fusion(f32[768,767]{1,0:T(8,128)} %copy-done.4, bf16[3072,767]{1,0:T(8,128)(2,1)} %all-gather.11.cloned.1.call-done, f32[767]{0:T(1024)S(1)} %copy-done.38, f32[768,3072]{1,0:T(8,128)} %fusion.51, f32[3072]{0:T(1024)} %param.23), kind=kOutput, calls=%fused_computation.55 | convolution fusion | flops 3644520192 | bytes 17699324 | tf_op jit(solution)/shard_map/dot_general | solution.py:114
  560.5 8.2 multiply_reduce_fusion.3
  568.7 39.5 %all-reduce = (f32[768]{0:T(1024)}, f32[12,128]{1,0:T(8,128)}, f32[767]{0:T(1024)}, f32[768]{0:T(1024)}, f32[3072]{0:T(1024)}, /*index=5*/f32[767]{0:T(1024)}) all-reduce(f32[768]{0:T(1024)} %get-tuple-element.14, f32[12,128]{1,0:T(8,128)} %pad_maximum_fusion.5, ...), channel_id=1, replica_groups=mesh['fsdp'=8,'seq'=4] {'fsdp','seq'}, use_global_device_ids=true, to_apply=%region_15.16 | all-reduce | flops 7678 | bytes 61424 | tf_op jit(solution)/shard_map/psum | solution.py:194
  610.6 34.1 %reduce-scatter.5.cloned.1.call-done = f32[96,2304]{1,0:T(8,128)} async-done(((f32[768,2304]{1,0:T(8,128)}), f32[96,2304]{1,0:T(8,128)}) %reduce-scatter.5.cloned.1.call-update) | async-done | bytes 884752 | tf_op jit(solution)/shard_map/reduce_scatter | solution.py:183
  646.6 164.6 %reduce-scatter.11.cloned.1.call-done = f32[384,767]{1,0:T(8,128)} async-done(((f32[3072,767]{1,0:T(8,128)}), f32[384,767]{1,0:T(8,128)}) %reduce-scatter.11.cloned.1.call-update) | async-done | bytes 1178128 | tf_op jit(solution)/shard_map/reduce_scatter | solution.py:186
  813.4 164.5 %reduce-scatter.9.cloned.1.call-done = f32[96,3072]{1,0:T(8,128)} async-done(((f32[768,3072]{1,0:T(8,128)}), f32[96,3072]{1,0:T(8,128)}) %reduce-scatter.9.cloned.1.call-update) | async-done | bytes 1179664 | tf_op jit(solution)/shard_map/reduce_scatter | solution.py:185
  984.6 42.9 %all-reduce.4.cloned.1.call-done = (bf16[96,2304]{1,0:T(8,128)(2,1)}, bf16[96,767]{1,0:T(8,128)(2,1)}, bf16[96,3072]{1,0:T(8,128)(2,1)}, bf16[384,767]{1,0:T(8,128)(2,1)}) async-done(((bf16[96,2304]{1,0:T(8,128)(2,1)}, bf16[96,767]{1,0:T(8,128)(2,1)}, bf16[96,3072]{1,0:T(8,128)(2,1)}, bf16[384,767]{1,0:T(8,128)(2,1)}), (bf16[96,2304]{1,0:T(8,128)(2,1)}, bf16[96,767]{1,0:T(8,128)(2,1)}, ...) | async-done | bytes 1768528 | tf_op jit(solution)/shard_map/psum | solution.py:189
  (164 shorter events, 73.4 us)
Async XLA Ops:
  7.2 4.0 copy-start.18
  7.2 4.9 copy-start.16
  7.2 71.5 %all-gather.5.cloned.1.call-start = ((), (), s32[]{:S(2)}) async-start(), calls=%async_computation.8 | async-start | bytes 3981312 | tf_op jit(solution)/shard_map/all_gather | solution.py:64
  9.4 3.1 copy-start.32
  9.4 251.2 %all-gather.7.cloned.1.call-start = ((), (), s32[]{:S(2)}) async-start(), calls=%async_computation.9 | async-start | bytes 1327104 | tf_op jit(solution)/shard_map/all_gather | solution.py:65
  11.1 254.5 %all-gather.9.cloned.1.call-start = ((), (), s32[]{:S(2)}) async-start(), calls=%async_computation.10 | async-start | bytes 5308416 | tf_op jit(solution)/shard_map/all_gather | solution.py:66
  12.9 65.9 %copy-start.9 = (f32[1,768]{0,1:T(8,128)}, f32[1,768]{0,1:T(8,128)S(1)}, u32[]{:S(2)}) copy-start(f32[1,768]{0,1:T(8,128)S(1)} %copy.93) | copy-start | bytes 9220
  12.9 65.8 %copy-start.26 = (f32[768]{0:T(1024)S(1)}, f32[768]{0:T(1024)}, u32[]{:S(2)}) copy-start(f32[768]{0:T(1024)} %param.16) | copy-start | bytes 9220
  14.5 70.8 %copy-start = (f32[768,767]{1,0:T(8,128)}, f32[768,767]{1,0:T(8,128)S(1)}, u32[]{:S(2)}) copy-start(f32[768,767]{1,0:T(8,128)S(1)} %convert.50) | copy-start | bytes 7068676
  15.6 69.7 %copy-start.23 = (f32[768]{0:T(1024)}, f32[768]{0:T(1024)S(1)}, u32[]{:S(2)}) copy-start(f32[768]{0:T(1024)S(1)} %fusion.47) | copy-start | bytes 9220
  102.3 45.0 %all-to-all-start = ((bf16[3,256,4,576]{1,3,0,2:T(8,128)(2,1)}), bf16[3,256,4,576]{1,3,0,2:T(8,128)(2,1)S(1)}, u32[]{:S(2)}, u32[]{:S(2)}) async-start(bf16[3,256,4,576]{1,3,0,2:T(8,128)(2,1)} %copy.69), calls=%async_computation | async-start | bytes 7077888 | tf_op jit(solution)/shard_map/all_to_all | solution.py:79
  106.1 2.2 copy-start.34
  106.1 175.9 %all-gather.11.cloned.1.call-start = ((), (), s32[]{:S(2)}) async-start(), calls=%async_computation.11 | async-start | bytes 5308416 | tf_op jit(solution)/shard_map/all_gather | solution.py:67
  157.8 1.9 copy-start.17
  158.0 11.0 %copy-start.13 = (bf16[3,1024,3,64]{1,3,2,0:T(8,128)(2,1)}, bf16[3,1024,3,64]{1,3,2,0:T(8,128)(2,1)S(1)}, u32[]{:S(2)}) copy-start(bf16[3,1024,3,64]{1,3,2,0:T(8,128)(2,1)S(1)} %slice_bitcast_fusion.1) | copy-start | bytes 3538948
  254.0 6.6 copy-start.37
  263.8 1.4 copy-start.4
  263.8 1.8 copy-start.25
  264.0 1.5 copy-start.11
  282.0 13.7 %copy-start.5 = (f32[768,767]{1,0:T(8,128)S(1)}, f32[768,767]{1,0:T(8,128)}, u32[]{:S(2)}) copy-start(f32[768,767]{1,0:T(8,128)} %copy-done.4) | copy-start | bytes 7068676
  282.0 13.7 %copy-start.12 = (f32[768,1]{1,0:T(8,128)S(1)}, f32[768,1]{1,0:T(8,128)}, u32[]{:S(2)}) copy-start(f32[768,1]{1,0:T(8,128)} %copy-done.11) | copy-start | bytes 9220
  282.0 13.7 %copy-start.35 = (bf16[768,3072]{1,0:T(8,128)(2,1)S(1)}, bf16[768,3072]{1,0:T(8,128)(2,1)}, u32[]{:S(2)}) copy-start(bf16[768,3072]{1,0:T(8,128)(2,1)} %all-gather.9.cloned.1.call-done) | copy-start | bytes 14155780
  295.7 4.8 copy-start.15
  300.5 1.3 copy-start.6
  301.1 1.7 copy-start.2
  301.8 1.1 copy-start.28
  301.8 2.1 copy-start.36
  314.0 20.2 %all-to-all-start.2 = ((bf16[3,256,4,192]{1,3,0,2:T(8,128)(2,1)}), bf16[3,256,4,192]{1,3,0,2:T(8,128)(2,1)}, u32[]{:S(2)}, u32[]{:S(2)}) async-start(bf16[3,256,4,192]{1,3,0,2:T(8,128)(2,1)} %copy.79), calls=%async_computation.2 | async-start | bytes 2359296 | tf_op jit(solution)/shard_map/all_to_all | solution.py:144
  318.3 290.7 %reduce-scatter.7.cloned.1.call-start = ((), (), s32[]{:S(2)}) async-start(), calls=%async_computation.13 | async-start | bytes 2654208 | tf_op jit(solution)/shard_map/reduce_scatter | solution.py:184
  325.2 319.5 %reduce-scatter.5.cloned.1.call-start = ((), (), s32[]{:S(2)}) async-start(), calls=%async_computation.12 | async-start | bytes 7962624 | tf_op jit(solution)/shard_map/reduce_scatter | solution.py:183
  341.2 8.6 copy-start.8
  341.2 8.7 copy-start.21
  349.9 15.7 %copy-start.22 = (f32[3,3,512]{2,1,0:T(4,128)S(1)}, f32[3,3,512]{2,1,0:T(4,128)}, u32[]{:S(2)}) copy-start(f32[3,3,512]{2,1,0:T(4,128)} %log_add_fusion.1) | copy-start | bytes 55300
  394.1 3.1 copy-start.14
  502.3 8.0 copy-start.1
  502.3 8.0 copy-start.10
  502.3 8.0 copy-start.24
  502.3 8.0 copy-start.27
  518.0 1.3 copy-start.7
  518.0 293.3 %reduce-scatter.11.cloned.1.call-start = ((), (), s32[]{:S(2)}) async-start(), calls=%async_computation.15 | async-start | bytes 10616832 | tf_op jit(solution)/shard_map/reduce_scatter | solution.py:186
  532.7 445.1 %reduce-scatter.9.cloned.1.call-start = ((), (), s32[]{:S(2)}) async-start(), calls=%async_computation.14 | async-start | bytes 10616832 | tf_op jit(solution)/shard_map/reduce_scatter | solution.py:185
  543.6 1.2 copy-start.38
  543.6 484.0 %all-reduce.4.cloned.1.call-start = ((), (), s32[]{:S(2)}) async-start(), calls=%async_computation.16 | async-start | bytes 3538944 | tf_op jit(solution)/shard_map/psum | solution.py:189
  560.5 8.2 copy-start.33
  560.5 47.7 %copy-start.31 = (f32[768]{0:T(1024)S(1)}, f32[768]{0:T(1024)}, u32[]{:S(2)}) copy-start(f32[768]{0:T(1024)} %copy-done.30) | copy-start | bytes 9220
  980.0 2.7 copy-start.3
  980.1 2.7 copy-start.29
  1027.6 5.9 copy-start.20
  (2 other events, 1.9 us)
Sparse Core Ops, SparseCore 0:
  10.8 67.8 all-gather.4
  81.5 39.5 all-gather.6
  123.2 78.6 all-gather.8
  204.0 77.9 all-gather.10
  325.3 67.4 reduce-scatter.6
  518.1 126.5 reduce-scatter.4
  648.7 162.5 reduce-scatter.10
  815.3 162.5 reduce-scatter.8
  981.8 45.7 all-reduce.3
where the time goes:
time: 1050 us; the launch traced here: 1040 us
  waiting for transfers between devices  518 us (49%)
  matrix products  194 us (18%)
  blocking collectives  131 us (12%)
  other arithmetic  96.7 us (9%)
  local copies, waits for them, and re-layouts  78 us (7%)
  between operations  14.8 us (1%)
    reduce_scatter x1, waiting for transfers between devices, local(): lax.psum_scatter(proj_grad, 'fsdp', scatter_dimension=0, tiled=True)  165 us
    reduce_scatter x1, waiting for transfers between devices, local(): lax.psum_scatter(fc_grad, 'fsdp', scatter_dimension=0, tiled=True)  164 us
    all_to_all x1, blocking collectives, local(): lax.all_to_all(d_packed, 'seq', split_axis=1, concat_axis=2, tiled=True)  63.3 us
    all_gather x1, waiting for transfers between devices, local(): lax.all_gather(qkv_weight.astype(jnp.bfloat16), 'fsdp', axis=0, tiled=True)  63.1 us
    psum x1, waiting for transfers between devices, local(): lax.psum(qkv_share.astype(jnp.bfloat16), 'seq').astype(jnp.float32)  42.9 us
    psum x1, blocking collectives, local(): lax.psum((gain_one_grad, qv_bias_grad, out_bias_grad, gain_two_grad, fc_b...  39.5 us
    all_to_all x1, waiting for transfers between devices, local(): lax.all_to_all(packed, 'seq', split_axis=2, concat_axis=1, tiled=True)  34.3 us
    reduce_scatter x1, waiting for transfers between devices, local(): lax.psum_scatter(qkv_grad, 'fsdp', scatter_dimension=0, tiled=True)  34.1 us
  transfers between devices with their start and end apart: 11, of which 8 were waited for; matrix products, arithmetic and copies ran while one was open for 31% of the time, Pallas kernels for 0%

commit v1 on v0

--- a/solution.py
+++ b/solution.py
@@ -103,7 +103,10 @@
         )
     attended = jnp.concatenate(outputs_list, axis=1).astype(jnp.bfloat16)
     attended = attended.reshape(seq_count, full_len, my_heads * head_dim)
-    by_tokens = lax.all_to_all(attended, "seq", split_axis=1, concat_axis=2, tiled=True)
+    by_tokens = jnp.concatenate(
+        lax.all_to_all(jnp.stack(jnp.split(attended, lax.axis_size("seq"), axis=1)), "seq", 0, 0),
+        axis=2,
+    )
     attn_flat = by_tokens.reshape(token_count, width)
     middle = (
         resid_flat + jnp.dot(attn_flat, out_matrix, preferred_element_type=jnp.float32) + out_bias

time: 1050 us -> 1050 us (level)
  waiting for transfers between devices: 518 us -> 535 us
    all_gather x1, waiting for transfers between devices: 5.49 us -> 22.7 us  [local(): lax.all_gather(proj_weight.astype(jnp.bfloat16), 'fsdp', axis=0, tiled=True)]
  transfers between devices with their start and end apart: 11 -> 11, of which waited for: 8 -> 8; matrix products, arithmetic and copies ran while one was open for 31% -> 30% of each run, Pallas kernels for 0% -> 0%
where the time goes in v1:
time: 1050 us; the launch traced here: 1040 us
  waiting for transfers between devices  535 us (51%)
  matrix products  192 us (18%)
  blocking collectives  122 us (12%)
  other arithmetic  94.1 us (9%)
  local copies, waits for them, and re-layouts  74.9 us (7%)
  between operations  14.6 us (1%)
    reduce_scatter x1, waiting for transfers between devices, local(): lax.psum_scatter(fc_grad, 'fsdp', scatter_dimension=0, tiled=True)  164 us
    reduce_scatter x1, waiting for transfers between devices, local(): lax.psum_scatter(proj_grad, 'fsdp', scatter_dimension=0, tiled=True)  164 us
    all_to_all x1, blocking collectives, local(): lax.all_to_all(d_packed, 'seq', split_axis=1, concat_axis=2, tiled=True)  63.3 us
    all_gather x1, waiting for transfers between devices, local(): lax.all_gather(qkv_weight.astype(jnp.bfloat16), 'fsdp', axis=0, tiled=True)  63.1 us
    psum x1, waiting for transfers between devices, local(): lax.psum(qkv_share.astype(jnp.bfloat16), 'seq').astype(jnp.float32)  42.9 us
    psum x1, blocking collectives, local(): lax.psum((gain_one_grad, qv_bias_grad, out_bias_grad, gain_two_grad, fc_b...  39.7 us
    all_to_all x1, waiting for transfers between devices, local(): lax.all_to_all(packed, 'seq', split_axis=2, concat_axis=1, tiled=True)  34.3 us
    reduce_scatter x1, waiting for transfers between devices, local(): lax.psum_scatter(qkv_grad, 'fsdp', scatter_dimension=0, tiled=True)  34 us
  transfers between devices with their start and end apart: 11, of which 8 were waited for; matrix products, arithmetic and copies ran while one was open for 30% of the time, Pallas kernels for 0%

profile of v1, /device:TPU:0, one launch (start us, length us, event | category | flops | bytes accessed | tf_op | source)
XLA Modules:
  0.0 1041.8 jit_solution(2397170289816866010)
XLA Ops:
  15.6 63.1 %all-gather.5.cloned.1.call-done = bf16[768,2304]{1,0:T(8,128)(2,1)} async-done(((bf16[96,2304]{1,0:T(8,128)(2,1)}), bf16[768,2304]{1,0:T(8,128)(2,1)}) %all-gather.5.cloned.1.call-update) | async-done | bytes 3538960 | tf_op jit(solution)/shard_map/all_gather | solution.py:64
  78.7 6.6 add_convert_fusion
  85.3 9.1 reshape.214
  94.4 7.8 copy.70
  102.3 3.7 all-to-all-start
  109.1 3.8 compare_and_fusion.1
  112.9 34.3 %all-to-all-done = bf16[3,256,4,576]{1,3,0,2:T(8,128)(2,1)S(1)} async-done(((bf16[3,256,4,576]{1,3,0,2:T(8,128)(2,1)}), bf16[3,256,4,576]{1,3,0,2:T(8,128)(2,1)S(1)}, u32[]{:S(2)}, u32[]{:S(2)}) %all-to-all-start) | async-done | bytes 3538976 | tf_op jit(solution)/shard_map/all_to_all | solution.py:79
  147.1 4.5 copy.71
  151.7 6.1 reshape.215
  159.7 9.2 fusion.57
  168.9 10.1 fusion.1
  179.0 8.5 fusion.28
  188.4 9.5 fusion.58
  197.9 10.0 fusion
  207.9 9.0 fusion.29
  217.1 19.4 %all_to_all.50 = bf16[4,3,256,192]{2,3,1,0:T(8,128)(2,1)} all-to-all(bf16[4,3,256,192]{2,3,1,0:T(8,128)(2,1)S(1)} %pad_maximum_fusion.3), channel_id=1, replica_groups=mesh['fsdp'=8,'seq'=4] {'seq'}, dimensions={0} | all-to-all | bytes 2359296 | tf_op jit(solution)/shard_map/all_to_all | solution.py:107
  236.5 3.7 copy.75
  240.2 4.0 reshape_reshape.3
  249.2 10.7 %fusion.51 = f32[768,3072]{1,0:T(8,128)} fusion(bf16[768,3072]{1,0:T(8,128)(2,1)} %all-gather.9.cloned.1.call-done, f32[768]{0:T(1024)S(1)} %copy-done.29, f32[768]{0:T(1024)S(1)} %fusion.48, f32[768,1]{1,0:T(8,128)} %copy-done.11, f32[768,767]{1,0:T(8,128)} %copy-done.4), kind=kOutput, calls=%fused_computation.121 | convolution fusion | flops 3626237952 | bytes 16521216 | tf_op jit(solution)/shard_map/dot_general | solution.py:115
  259.9 22.7 %all-gather.11.cloned.1.call-done = bf16[3072,767]{1,0:T(8,128)(2,1)} async-done(((bf16[384,767]{1,0:T(8,128)(2,1)}), bf16[3072,767]{1,0:T(8,128)(2,1)}) %all-gather.11.cloned.1.call-update) | async-done | bytes 4712464 | tf_op jit(solution)/shard_map/all_gather | solution.py:67
  282.6 13.7 %convert_reduce_fusion = (f32[3072]{0:T(1024)}, bf16[768,3072]{1,0:T(8,128)(2,1)S(1)}) fusion(f32[768,3072]{1,0:T(8,128)} %fusion.51, f32[3072]{0:T(1024)} %param.23, bf16[768,767]{1,0:T(8,128)(2,1)} %bitcast.121, bf16[3072,767]{1,0:T(8,128)(2,1)} %all-gather.11.cloned.1.call-done), kind=kOutput, calls=%fused_computation.27 | convolution fusion | flops 3673420800 | bytes 20070912 | tf_op jit(solution)/shard_map/tc,fc->tf/dot_general | solution.py:129
  296.3 4.8 multiply_reduce_fusion.2
  306.6 4.4 reshape.219
  311.0 3.5 copy.77
  314.6 4.3 all-to-all-start.2
  321.7 4.1 fusion.60
  325.9 8.9 all-to-all-done.2
  338.0 3.6 reshape.220
  341.6 8.6 fusion.11
  350.3 15.7 %multiply_reduce_fusion = (f32[3,3,512]{2,1,0:T(4,128)S(1)}, f32[3,3,512,1024]{3,2,1,0:T(8,128)}) fusion(f32[3,3,512,1024]{3,2,1,0:T(8,128)} %get-tuple-element.45, f32[3,3,512]{2,1,0:T(4,128)S(1)} %copy-done.25, bf16[3,1024,3,3,64]{1,4,3,2,0:T(8,128)(2,1)S(1)} %reshape.215, bf16[3,1024,3,64]{1,3,2,0:T(8,128)(2,1)S(1)} %copy-done.8), kind=kOutput, calls=%fused_computation.1 | convolution fusion | flops 618130944 | bytes 39561216 | tf_op jit(solution)/shard_map/bqhe,bkhe->bhqk/dot_general | solution.py:158
  366.0 15.5 %multiply_reduce_fusion.1 = (f32[3,3,512]{2,1,0:T(4,128)S(1)}, f32[3,3,512,1024]{3,2,1,0:T(8,128)}) fusion(f32[3,3,512,1024]{3,2,1,0:T(8,128)} %get-tuple-element.47, f32[3,3,512]{2,1,0:T(4,128)S(1)} %copy-done.26, bf16[3,1024,3,3,64]{1,4,3,2,0:T(8,128)(2,1)S(1)} %reshape.215, bf16[3,1024,3,64]{1,3,2,0:T(8,128)(2,1)S(1)} %copy-done.8), kind=kOutput, calls=%fused_computation.4 | convolution fusion | flops 618130944 | bytes 39561216 | tf_op jit(solution)/shard_map/bqhe,bkhe->bhqk/dot_general | solution.py:158
  381.4 13.1 %multiply_convert_fusion.1 = bf16[3,3,512,1024]{3,2,1,0:T(8,128)(2,1)S(1)} fusion(f32[3,3,512,1024]{3,2,1,0:T(8,128)} %get-tuple-element.52, f32[3,3,512,1024]{3,2,1,0:T(8,128)} %get-tuple-element.47, f32[3,3,512]{2,1,0:T(4,128)S(1)} %get-tuple-element.51, f32[3,3,512]{2,1,0:T(4,128)S(1)} %copy-done.26), kind=kLoop, calls=%fused_computation.3 | loop fusion | flops 18874368 | bytes 47222784 | tf_op jit(solution)/shard_map/convert_element_type | solution.py:162
  399.4 8.3 fusion.24
  407.7 13.3 %multiply_convert_fusion = bf16[3,3,512,1024]{3,2,1,0:T(8,128)(2,1)S(1)} fusion(f32[3,3,512,1024]{3,2,1,0:T(8,128)} %get-tuple-element.54, f32[3,3,512,1024]{3,2,1,0:T(8,128)} %get-tuple-element.45, f32[3,3,512]{2,1,0:T(4,128)S(1)} %get-tuple-element.53, f32[3,3,512]{2,1,0:T(4,128)S(1)} %copy-done.25), kind=kLoop, calls=%fused_computation | loop fusion | flops 18874368 | bytes 47222784 | tf_op jit(solution)/shard_map/convert_element_type | solution.py:162
  426.9 6.3 copy.80
  433.1 63.3 %all_to_all.51 = bf16[3,1024,576]{2,0,1:T(4,128)(2,1)S(1)} all-to-all(bf16[3,1024,576]{2,0,1:T(4,128)(2,1)} %copy.80), channel_id=1, replica_groups=mesh['fsdp'=8,'seq'=4] {'seq'}, dimensions={1} | all-to-all | bytes 7077888 | tf_op jit(solution)/shard_map/all_to_all | solution.py:176
  496.4 6.7 convert_reduce_fusion.1
  503.1 8.0 reshape.221
  511.0 7.6 fusion.49
  519.9 13.4 %fusion.52 = f32[3072,767]{1,0:T(8,128)} fusion(bf16[768,767]{1,0:T(8,128)(2,1)S(1)} %bitcast.122, f32[768,3072]{1,0:T(8,128)} %fusion.51, f32[3072]{0:T(1024)} %param.23), kind=kOutput, calls=%fused_computation.122 | convolution fusion | flops 3642753024 | bytes 20052480 | tf_op jit(solution)/shard_map/tf,tc->fc/dot_general | solution.py:127
  533.5 10.8 %fusion.50 = f32[768,3072]{1,0:T(8,128)} fusion(bf16[768,3072]{1,0:T(8,128)(2,1)} %copy-done.16, f32[768]{0:T(1024)S(1)} %copy-done.29, f32[768]{0:T(1024)S(1)} %fusion.48, f32[768,1]{1,0:T(8,128)} %copy-done.11, f32[768,767]{1,0:T(8,128)} %copy-done.4), kind=kOutput, calls=%fused_computation.120 | convolution fusion | flops 3626237952 | bytes 16521216 | tf_op jit(solution)/shard_map/td,tf->df/dot_general | solution.py:132
  545.4 12.8 %add_convert_fusion.2 = bf16[768,767]{1,0:T(8,128)(2,1)} fusion(f32[768,767]{1,0:T(8,128)} %copy-done.4, bf16[3072,767]{1,0:T(8,128)(2,1)} %all-gather.11.cloned.1.call-done, f32[767]{0:T(1024)S(1)} %copy-done.42, f32[768,3072]{1,0:T(8,128)} %fusion.51, f32[3072]{0:T(1024)} %param.23), kind=kOutput, calls=%fused_computation.55 | convolution fusion | flops 3644520192 | bytes 17699324 | tf_op jit(solution)/shard_map/dot_general | solution.py:117
  561.2 8.2 multiply_reduce_fusion.3
  569.4 39.7 %all-reduce = (f32[768]{0:T(1024)}, f32[12,128]{1,0:T(8,128)}, f32[767]{0:T(1024)}, f32[768]{0:T(1024)}, f32[3072]{0:T(1024)}, /*index=5*/f32[767]{0:T(1024)}) all-reduce(f32[768]{0:T(1024)} %get-tuple-element.14, f32[12,128]{1,0:T(8,128)} %pad_maximum_fusion.5, ...), channel_id=1, replica_groups=mesh['fsdp'=8,'seq'=4] {'fsdp','seq'}, use_global_device_ids=true, to_apply=%region_15.16 | all-reduce | flops 7678 | bytes 61424 | tf_op jit(solution)/shard_map/psum | solution.py:197
  611.4 34.0 %reduce-scatter.5.cloned.1.call-done = f32[96,2304]{1,0:T(8,128)} async-done(((f32[768,2304]{1,0:T(8,128)}), f32[96,2304]{1,0:T(8,128)}) %reduce-scatter.5.cloned.1.call-update) | async-done | bytes 884752 | tf_op jit(solution)/shard_map/reduce_scatter | solution.py:186
  647.4 164.4 %reduce-scatter.11.cloned.1.call-done = f32[384,767]{1,0:T(8,128)} async-done(((f32[3072,767]{1,0:T(8,128)}), f32[384,767]{1,0:T(8,128)}) %reduce-scatter.11.cloned.1.call-update) | async-done | bytes 1178128 | tf_op jit(solution)/shard_map/reduce_scatter | solution.py:189
  813.9 164.5 %reduce-scatter.9.cloned.1.call-done = f32[96,3072]{1,0:T(8,128)} async-done(((f32[768,3072]{1,0:T(8,128)}), f32[96,3072]{1,0:T(8,128)}) %reduce-scatter.9.cloned.1.call-update) | async-done | bytes 1179664 | tf_op jit(solution)/shard_map/reduce_scatter | solution.py:188
  985.2 42.9 %all-reduce.4.cloned.1.call-done = (bf16[96,2304]{1,0:T(8,128)(2,1)}, bf16[96,767]{1,0:T(8,128)(2,1)}, bf16[96,3072]{1,0:T(8,128)(2,1)}, bf16[384,767]{1,0:T(8,128)(2,1)}) async-done(((bf16[96,2304]{1,0:T(8,128)(2,1)}, bf16[96,767]{1,0:T(8,128)(2,1)}, bf16[96,3072]{1,0:T(8,128)(2,1)}, bf16[384,767]{1,0:T(8,128)(2,1)}), (bf16[96,2304]{1,0:T(8,128)(2,1)}, bf16[96,767]{1,0:T(8,128)(2,1)}, ...) | async-done | bytes 1768528 | tf_op jit(solution)/shard_map/psum | solution.py:192
  (172 shorter events, 67.0 us)
Async XLA Ops:
  7.2 4.0 copy-start.22
  7.2 4.9 copy-start.17
  7.2 71.5 %all-gather.5.cloned.1.call-start = ((), (), s32[]{:S(2)}) async-start(), calls=%async_computation.8 | async-start | bytes 3981312 | tf_op jit(solution)/shard_map/all_gather | solution.py:64
  9.4 3.0 copy-start.36
  9.4 234.8 %all-gather.7.cloned.1.call-start = ((), (), s32[]{:S(2)}) async-start(), calls=%async_computation.9 | async-start | bytes 1327104 | tf_op jit(solution)/shard_map/all_gather | solution.py:65
  11.1 238.1 %all-gather.9.cloned.1.call-start = ((), (), s32[]{:S(2)}) async-start(), calls=%async_computation.10 | async-start | bytes 5308416 | tf_op jit(solution)/shard_map/all_gather | solution.py:66
  12.9 65.9 %copy-start.9 = (f32[1,768]{0,1:T(8,128)}, f32[1,768]{0,1:T(8,128)S(1)}, u32[]{:S(2)}) copy-start(f32[1,768]{0,1:T(8,128)S(1)} %copy.89) | copy-start | bytes 9220
  12.9 65.8 %copy-start.30 = (f32[768]{0:T(1024)S(1)}, f32[768]{0:T(1024)}, u32[]{:S(2)}) copy-start(f32[768]{0:T(1024)} %param.16) | copy-start | bytes 9220
  14.5 70.8 %copy-start = (f32[768,767]{1,0:T(8,128)}, f32[768,767]{1,0:T(8,128)S(1)}, u32[]{:S(2)}) copy-start(f32[768,767]{1,0:T(8,128)S(1)} %convert.50) | copy-start | bytes 7068676
  15.6 69.7 %copy-start.27 = (f32[768]{0:T(1024)}, f32[768]{0:T(1024)S(1)}, u32[]{:S(2)}) copy-start(f32[768]{0:T(1024)S(1)} %fusion.47) | copy-start | bytes 9220
  102.3 44.9 %all-to-all-start = ((bf16[3,256,4,576]{1,3,0,2:T(8,128)(2,1)}), bf16[3,256,4,576]{1,3,0,2:T(8,128)(2,1)S(1)}, u32[]{:S(2)}, u32[]{:S(2)}) async-start(bf16[3,256,4,576]{1,3,0,2:T(8,128)(2,1)} %copy.70), calls=%async_computation | async-start | bytes 7077888 | tf_op jit(solution)/shard_map/all_to_all | solution.py:79
  106.0 2.2 copy-start.38
  106.0 176.6 %all-gather.11.cloned.1.call-start = ((), (), s32[]{:S(2)}) async-start(), calls=%async_computation.11 | async-start | bytes 5308416 | tf_op jit(solution)/shard_map/all_gather | solution.py:67
  157.7 2.0 copy-start.19
  157.9 11.1 %copy-start.13 = (bf16[3,1024,3,64]{1,3,2,0:T(8,128)(2,1)}, bf16[3,1024,3,64]{1,3,2,0:T(8,128)(2,1)S(1)}, u32[]{:S(2)}) copy-start(bf16[3,1024,3,64]{1,3,2,0:T(8,128)(2,1)S(1)} %slice_bitcast_fusion.1) | copy-start | bytes 3538948
  179.0 9.4 copy-start.14
  179.0 9.4 copy-start.18
  207.9 9.0 copy-start.20
  207.9 9.0 copy-start.21
  236.5 7.7 copy-start.41
  247.4 1.4 copy-start.4
  247.4 1.8 copy-start.29
  247.6 1.5 copy-start.11
  282.6 13.7 %copy-start.5 = (f32[768,767]{1,0:T(8,128)S(1)}, f32[768,767]{1,0:T(8,128)}, u32[]{:S(2)}) copy-start(f32[768,767]{1,0:T(8,128)} %copy-done.4) | copy-start | bytes 7068676
  282.6 13.7 %copy-start.12 = (f32[768,1]{1,0:T(8,128)S(1)}, f32[768,1]{1,0:T(8,128)}, u32[]{:S(2)}) copy-start(f32[768,1]{1,0:T(8,128)} %copy-done.11) | copy-start | bytes 9220
  282.6 13.7 %copy-start.39 = (bf16[768,3072]{1,0:T(8,128)(2,1)S(1)}, bf16[768,3072]{1,0:T(8,128)(2,1)}, u32[]{:S(2)}) copy-start(bf16[768,3072]{1,0:T(8,128)(2,1)} %all-gather.9.cloned.1.call-done) | copy-start | bytes 14155780
  296.3 4.8 copy-start.16
  301.7 1.7 copy-start.2
  302.4 2.1 copy-start.40
  314.6 20.2 %all-to-all-start.2 = ((bf16[3,256,4,192]{1,3,0,2:T(8,128)(2,1)}), bf16[3,256,4,192]{1,3,0,2:T(8,128)(2,1)}, u32[]{:S(2)}, u32[]{:S(2)}) async-start(bf16[3,256,4,192]{1,3,0,2:T(8,128)(2,1)} %copy.77), calls=%async_computation.2 | async-start | bytes 2359296 | tf_op jit(solution)/shard_map/all_to_all | solution.py:147
  318.9 290.9 %reduce-scatter.7.cloned.1.call-start = ((), (), s32[]{:S(2)}) async-start(), calls=%async_computation.13 | async-start | bytes 2654208 | tf_op jit(solution)/shard_map/reduce_scatter | solution.py:187
  325.8 319.6 %reduce-scatter.5.cloned.1.call-start = ((), (), s32[]{:S(2)}) async-start(), calls=%async_computation.12 | async-start | bytes 7962624 | tf_op jit(solution)/shard_map/reduce_scatter | solution.py:186
  341.6 8.7 copy-start.8
  341.6 8.7 copy-start.25
  350.2 15.7 %copy-start.26 = (f32[3,3,512]{2,1,0:T(4,128)S(1)}, f32[3,3,512]{2,1,0:T(4,128)}, u32[]{:S(2)}) copy-start(f32[3,3,512]{2,1,0:T(4,128)} %log_add_fusion.1) | copy-start | bytes 55300
  394.5 3.1 copy-start.15
  503.1 8.0 copy-start.1
  503.1 8.0 copy-start.10
  503.1 8.0 copy-start.28
  503.1 8.0 copy-start.31
  518.7 293.1 %reduce-scatter.11.cloned.1.call-start = ((), (), s32[]{:S(2)}) async-start(), calls=%async_computation.15 | async-start | bytes 10616832 | tf_op jit(solution)/shard_map/reduce_scatter | solution.py:189
  533.4 445.0 %reduce-scatter.9.cloned.1.call-start = ((), (), s32[]{:S(2)}) async-start(), calls=%async_computation.14 | async-start | bytes 10616832 | tf_op jit(solution)/shard_map/reduce_scatter | solution.py:188
  544.3 483.8 %all-reduce.4.cloned.1.call-start = ((), (), s32[]{:S(2)}) async-start(), calls=%async_computation.16 | async-start | bytes 3538944 | tf_op jit(solution)/shard_map/psum | solution.py:192
  561.1 8.2 copy-start.37
  561.1 47.9 %copy-start.35 = (f32[768]{0:T(1024)S(1)}, f32[768]{0:T(1024)}, u32[]{:S(2)}) copy-start(f32[768]{0:T(1024)} %copy-done.34) | copy-start | bytes 9220
  980.6 2.7 copy-start.3
  980.6 2.7 copy-start.33
  1028.1 5.9 copy-start.24
  (6 other events, 6.5 us)
Sparse Core Ops, SparseCore 0:
  10.8 67.8 all-gather.4
  80.9 39.5 all-gather.6
  123.2 78.6 all-gather.8
  204.5 78.0 all-gather.10
  326.0 67.6 reduce-scatter.6
  518.8 126.5 reduce-scatter.4
  649.4 162.3 reduce-scatter.10
  815.8 162.5 reduce-scatter.8
  982.4 45.6 all-reduce.3
